TPU v7x, 32 devices: a whole 2x2x4 slice. The times are simulated.
32 devices in a mesh: tx: 2 (over core), ty: 4 (over y, x), lz: 4 (over z).
Axes of the slice: x: 2, y: 2, z: 4, core: 2. Of those that a mesh axis runs over, the one named last changes fastest.
Arguments:
- test_field: bfloat16 [64, 6, 48, 512], P('tx', None, 'lz', 'ty'), may hold values from -6 to 6
- dir_field: bfloat16 [64, 6, 48, 512], P('tx', None, 'lz', 'ty'), may hold values from -6 to 6
- border_b: bfloat16 [64, 6, 48, 512], P('tx', None, 'lz', 'ty')
- border_c: bfloat16 [64, 6, 48, 512], P('tx', None, 'lz', 'ty')
- land_mask: int32 [64, 512], P('tx', 'ty'), may hold values from 0 to 1, as said below
- active_rows: int32 [64, 4], P('tx', 'ty'), may hold values from -1 to 31, as said below
- cell_blocks: bfloat16 [64, 36, 512], P('tx', None, 'ty'), may hold values from -2.5 to 2.5
- column_k: bfloat16 [288, 288], replicated, may hold values from -0.375 to 0.375
- kappa: float32 [6], replicated, may hold values from 0.2 to 1
Outputs:
- test_image: bfloat16 [64, 6, 48, 512], P('tx', None, 'lz', 'ty')
- dir_image: bfloat16 [64, 6, 48, 512], P('tx', None, 'lz', 'ty')
- border: float32 [3], replicated
Inputs may be any that keep to these rules, and one draw needn't show every extreme that they name: `active_rows`: in each tile the 32 entries name distinct local rows, the active ones, followed by -1 for the rest; some tile has all 32 rows active. `land_mask`: cells whose latitude index y has y % 128 equal to 0 or 127 are ocean.
All inputs are finite; a program needn't handle non-finite values.
Results may differ from a plain program's by a relative error of at most 0.0028.
Values may be sent and summed in bfloat16 or wider, within the bound.
A program may use at most 192 MiB of HBM per device.

v0:
```python
import jax
import jax.numpy as jnp
from jax import lax
from jax.sharding import PartitionSpec as P


def extended(value, sides, width, wrap):
    for axis, dim in sides:
        size, length = (lax.axis_size(axis), value.shape[dim])
        up = [(i, (i + 1) % size) for i in range(size if wrap else size - 1)]
        down = [(j, i) for i, j in up]
        last = lax.slice_in_dim(value, length - width, length, axis=dim)
        initial = lax.slice_in_dim(value, 0, width, axis=dim)
        before = lax.ppermute(last, axis, up)
        after = lax.ppermute(initial, axis, down)
        value = jnp.concatenate([before, value, after], axis=dim)
    return value


def body(
    test_field, dir_field, border_b, border_c, land_mask, active_rows, cell_blocks, column_k, kappa
):
    rows_here, units, layers, cells = test_field.shape
    col_size = column_k.shape[0]
    depth = col_size // units
    lines = jnp.arange(rows_here, dtype=jnp.int32)
    named = jnp.any(active_rows[:, 0][None, :] == lines[:, None], axis=1)
    weight = land_mask.astype(jnp.float32) * named.astype(jnp.float32)[:, None]
    stacked = jnp.concatenate(
        [
            test_field * weight.astype(jnp.bfloat16)[:, None, None, :],
            dir_field * weight.astype(jnp.bfloat16)[:, None, None, :],
        ],
        axis=1,
    )
    column_b = border_b.astype(jnp.float32)
    row_c = border_c.astype(jnp.float32)
    norm_b = jnp.sum(column_b * column_b)
    norm_c = jnp.sum(row_c * row_c)
    value_c = jnp.sum(row_c * test_field.astype(jnp.float32))
    part = lax.all_to_all(stacked, "lz", split_axis=0, concat_axis=2, tiled=True)
    group = part.shape[0]
    span = part.shape[3]
    flat = part.reshape(group, 2, col_size, span)
    product = jnp.einsum("pq,gfqc->gfpc", column_k, flat, preferred_element_type=jnp.float32)
    product = product.astype(jnp.bfloat16).reshape(group, 2 * units, depth, span)
    coupled = lax.all_to_all(product, "lz", split_axis=2, concat_axis=0, tiled=True).astype(
        jnp.float32
    )
    lon_padded = extended(stacked, (("tx", 0),), 1, True)
    lat_padded = extended(stacked, (("ty", 3),), 1, False)
    center = stacked.astype(jnp.float32)
    spread = (
        lon_padded[2:].astype(jnp.float32)
        + lon_padded[:-2].astype(jnp.float32)
        + lat_padded[..., 2:].astype(jnp.float32)
        + lat_padded[..., :-2].astype(jnp.float32)
        - 4.0 * center
    )
    rates = jnp.concatenate([kappa, kappa]).reshape(1, 2 * units, 1, 1)
    blocks = cell_blocks.reshape(rows_here, units, units, cells)
    local = jnp.einsum(
        "xuwy,xfwzy->xfuzy",
        blocks,
        stacked.reshape(rows_here, 2, units, layers, cells),
        preferred_element_type=jnp.float32,
    ).reshape(rows_here, 2 * units, layers, cells)
    image = weight[:, None, None, :] * (coupled + local + rates * spread)
    test_full = image[:, :units]
    dir_full = image[:, units:]
    value_a = jnp.sum(column_b * test_full)
    value_e = jnp.sum(column_b * dir_full)
    norm_b, norm_c, value_c, value_a, value_e = lax.psum(
        (norm_b, norm_c, value_c, value_a, value_e), ("tx", "ty", "lz")
    )
    border = jnp.stack(
        [value_a / jnp.sqrt(norm_b), value_e / jnp.sqrt(norm_b), value_c / jnp.sqrt(norm_c)]
    )
    return (test_full.astype(jnp.bfloat16), dir_full.astype(jnp.bfloat16), border)


def solution(mesh):
    in_specs = (
        P("tx", None, "lz", "ty"),
        P("tx", None, "lz", "ty"),
        P("tx", None, "lz", "ty"),
        P("tx", None, "lz", "ty"),
        P("tx", "ty"),
        P("tx", "ty"),
        P("tx", None, "ty"),
        P(),
        P(),
    )
    out_specs = (P("tx", None, "lz", "ty"), P("tx", None, "lz", "ty"), P())
    return jax.shard_map(body, mesh=mesh, in_specs=in_specs, out_specs=out_specs, check_vma=False)
```

profile of v0, /device:TPU:0, one launch (start us, length us, event | category | flops | bytes accessed | tf_op | source)
XLA Modules:
  0.0 150.9 jit_solution(9420423562500274029)
XLA Ops:
  2.3 1.3 broadcast_multiply_fusion.1
  3.7 1.7 %copy.43 = bf16[32,12,12,128]{3,2,1,0:T(8,128)(2,1)} copy(bf16[32,12,12,128]{3,0,2,1:T(8,128)(2,1)S(1)} %pad_maximum_fusion) | data formatting | bytes 2359296 | tf_op jit(solution)/shard_map/concatenate | solution.py:29
  5.4 6.3 %all-to-all-start = ((bf16[32,12,12,128]{3,2,1,0:T(8,128)(2,1)}), bf16[32,12,12,128]{3,2,1,0:T(8,128)(2,1)}, u32[]{:S(2)}, u32[]{:S(2)}) async-start(bf16[32,12,12,128]{3,2,1,0:T(8,128)(2,1)} %copy.43), calls=%async_computation | async-start | bytes 3145728 | tf_op jit(solution)/shard_map/all_to_all | solution.py:41
  11.7 1.9 %fusion.7 = (bf16[32,12,12,1]{3,0,2,1:T(8,128)(2,1)}, bf16[32,12,12,1]{3,0,2,1:T(8,128)(2,1)}) fusion(bf16[32,6,12,128]{3,0,2,1:T(8,128)(2,1)S(1)} %get-tuple-element.21, bf16[32,6,12,128]{3,0,2,1:T(8,128)(2,1)S(1)} %get-tuple-element.22), kind=kLoop, calls=%fused_computation.25 | loop fusion | flops 9216 | bytes 1198080 | tf_op jit(solution)/shard_map/concatenate | solution.py:29
  13.6 2.4 %copy.53 = bf16[32,12,12,1]{0,2,3,1:T(8,128)(2,1)S(1)} copy(bf16[32,12,12,1]{3,0,2,1:T(8,128)(2,1)} %get-tuple-element.19) | data formatting | bytes 18432 | tf_op jit(solution)/shard_map/slice | solution.py:13
  16.0 1.3 collective-permute-start.2
  17.3 2.5 %copy.55 = bf16[32,12,12,1]{0,2,3,1:T(8,128)(2,1)S(1)} copy(bf16[32,12,12,1]{3,0,2,1:T(8,128)(2,1)} %get-tuple-element.20) | data formatting | bytes 18432 | tf_op jit(solution)/shard_map/slice | solution.py:12
  19.8 4.6 %collective-permute-start.3 = (bf16[32,12,12,1]{0,2,3,1:T(8,128)(2,1)S(1)}, bf16[32,12,12,1]{0,2,3,1:T(8,128)(2,1)S(1)}, u32[]{:S(2)}, u32[]{:S(2)}) collective-permute-start(bf16[32,12,12,1]{0,2,3,1:T(8,128)(2,1)S(1)} %copy.55), channel_id=1, source_target_pairs={{0,4},{4,8},{8,12},{1,5},{5,9},{9,13},{2,6},{6,10},{10,14},{3,7},{... | collective-permute-start | bytes 27656 | tf_op jit(solution)/shard_map/ppermute | solution.py:14
  25.1 10.2 %copy.50 = bf16[32,2,6,12,128]{3,2,1,4,0:T(8,128)(2,1)} copy(bf16[32,2,6,12,128]{4,0,3,2,1:T(8,128)(2,1)S(1)} %bitcast.37) | data formatting | bytes 2359296 | tf_op jit(solution)/shard_map/reshape | solution.py:65
  35.3 5.5 %copy.58 = bf16[32,6,6,128,1]{2,1,4,3,0:T(8,128)(2,1)} copy(bf16[32,6,6,128,1]{3,0,2,1,4:T(8,128)(2,1)S(1)} %bitcast.41) | data formatting | bytes 589824 | tf_op jit(solution)/shard_map/reshape | solution.py:61
  40.8 1.0 fusion.3
  41.8 7.0 %all-to-all-done = bf16[32,12,12,128]{3,2,1,0:T(8,128)(2,1)} async-done(((bf16[32,12,12,128]{3,2,1,0:T(8,128)(2,1)}), bf16[32,12,12,128]{3,2,1,0:T(8,128)(2,1)}, u32[]{:S(2)}, u32[]{:S(2)}) %all-to-all-start) | async-done | bytes 1179680 | tf_op jit(solution)/shard_map/all_to_all | solution.py:41
  48.8 2.8 %copy.45 = bf16[8,12,4,12,128]{4,0,3,2,1:T(8,128)(2,1)S(1)} copy(bf16[8,12,4,12,128]{4,3,1,0,2:T(8,128)(2,1)} %bitcast.3) | data formatting | bytes 2359296 | tf_op jit(solution)/shard_map/all_to_all | solution.py:41
  52.4 1.9 %copy.47 = bf16[8,12,48,128]{3,0,1,2:T(8,128)(2,1)} copy(bf16[8,12,48,128]{3,2,1,0:T(8,128)(2,1)S(1)} %bitcast.39) | data formatting | bytes 2359296 | tf_op jit(solution)/shard_map/reshape | solution.py:46
  54.2 4.5 %all-to-all-start.1 = ((bf16[8,12,48,128]{3,0,1,2:T(8,128)(2,1)}), bf16[8,12,48,128]{3,0,1,2:T(8,128)(2,1)}, u32[]{:S(2)}, u32[]{:S(2)}) async-start(bf16[8,12,48,128]{3,0,1,2:T(8,128)(2,1)} %copy.47), calls=%async_computation.1 | async-start | bytes 2359296 | tf_op jit(solution)/shard_map/all_to_all | solution.py:47
  58.7 20.0 %convolution_bitcast_fusion = f32[32,2,6,12,128]{3,2,1,4,0:T(8,128)} fusion(bf16[32,2,6,12,128]{3,2,1,4,0:T(8,128)(2,1)} %copy.50, bf16[32,6,6,128,1]{2,1,4,3,0:T(8,128)(2,1)} %copy.58), kind=kOutput, calls=%fused_computation | convolution fusion | flops 7077888 | bytes 3833856 | tf_op jit(solution)/shard_map/xuwy,xfwzy->xfuzy/dot_general | solution.py:62
  78.8 15.6 %copy.52 = f32[32,2,6,12,128]{4,0,3,2,1:T(8,128)} copy(f32[32,2,6,12,128]{3,2,1,4,0:T(8,128)} %convolution_bitcast_fusion) | data formatting | bytes 4718592 | tf_op jit(solution)/shard_map/xuwy,xfwzy->xfuzy/transpose | solution.py:62
  94.4 1.0 copy.54
  95.4 1.9 %copy.56 = bf16[32,12,12,1]{3,0,2,1:T(8,128)(2,1)} copy(bf16[32,12,12,1]{0,2,3,1:T(8,128)(2,1)S(1)} %collective-permute-done.3) | data formatting | bytes 18432 | tf_op jit(solution)/shard_map/ppermute | solution.py:14
  97.3 1.6 %copy.48 = bf16[8,12,48,128]{3,0,2,1:T(8,128)(2,1)S(1)} copy(bf16[8,12,48,128]{3,0,1,2:T(8,128)(2,1)} %all-to-all-done.1) | data formatting | bytes 2359296 | tf_op jit(solution)/shard_map/all_to_all | solution.py:47
  99.0 4.8 %fusion.1 = f32[32,12,12,128]{3,0,2,1:T(8,128)S(1)} fusion(f32[32,2,6,12,128]{4,0,3,2,1:T(8,128)} %copy.52, bf16[32,12,12,1]{3,0,2,1:T(8,128)(2,1)S(1)} %copy-done.2, bf16[32,6,12,128]{3,0,2,1:T(8,128)(2,1)S(1)} %get-tuple-element.22, bf16[32,6,12,128]{3,0,2,1:T(8,128)(2,1)S(1)} %get-tuple-element.21, bf16[32,12,12,1]{3,0,2,1:T(8,128)(2,1)S(1)} %copy.54, ...), kind=kLoop, calls=%fused_computation.4 | loop fusion | flops 22413312 | bytes 7186480 | tf_op jit(solution)/shard_map/mul | solution.py:68
  103.8 1.3 fusion.15
  105.1 1.1 fusion.4
  106.2 40.9 %all-reduce = (f32[]{:T(128)}, f32[]{:T(128)}, f32[]{:T(128)}, f32[]{:T(128)}, f32[]{:T(128)}) all-reduce(f32[]{:T(128)} %get-tuple-element.7, f32[]{:T(128)} %get-tuple-element.6, f32[]{:T(128)} %get-tuple-element.4, f32[]{:T(128)} %get-tuple-element.5, f32[]{:T(128)} %get-tuple-element.3), channel_id=1, replica_groups=mesh['tx'=2,'ty'=4,'lz'=4] {'tx','ty','lz'}, use_global_device_ids=true, to_apply=%region_8.0 | all-reduce | flops 5 | bytes 40 | tf_op jit(solution)/shard_map/psum | solution.py:73
  (31 shorter events, 3.9 us)
Async XLA Ops:
  0.6 50.9 %copy-start = (bf16[288,288]{1,0:T(8,128)(2,1)S(1)}, bf16[288,288]{1,0:T(8,128)(2,1)}, u32[]{:S(2)}) copy-start(bf16[288,288]{1,0:T(8,128)(2,1)} %param.16) | copy-start | bytes 497668
  5.4 43.4 %all-to-all-start = ((bf16[32,12,12,128]{3,2,1,0:T(8,128)(2,1)}), bf16[32,12,12,128]{3,2,1,0:T(8,128)(2,1)}, u32[]{:S(2)}, u32[]{:S(2)}) async-start(bf16[32,12,12,128]{3,2,1,0:T(8,128)(2,1)} %copy.43), calls=%async_computation | async-start | bytes 3145728 | tf_op jit(solution)/shard_map/all_to_all | solution.py:41
  16.0 78.4 %collective-permute-start.2 = (bf16[32,12,12,1]{0,2,3,1:T(8,128)(2,1)S(1)}, bf16[32,12,12,1]{0,2,3,1:T(8,128)(2,1)S(1)}, u32[]{:S(2)}, u32[]{:S(2)}) collective-permute-start(bf16[32,12,12,1]{0,2,3,1:T(8,128)(2,1)S(1)} %copy.53), channel_id=1, source_target_pairs={{4,0},{8,4},{12,8},{5,1},{9,5},{13,9},{6,2},{10,6},{14,10},{7,3},{... | collective-permute-start | bytes 27656 | tf_op jit(solution)/shard_map/ppermute | solution.py:15
  19.8 75.6 %collective-permute-start.3 = (bf16[32,12,12,1]{0,2,3,1:T(8,128)(2,1)S(1)}, bf16[32,12,12,1]{0,2,3,1:T(8,128)(2,1)S(1)}, u32[]{:S(2)}, u32[]{:S(2)}) collective-permute-start(bf16[32,12,12,1]{0,2,3,1:T(8,128)(2,1)S(1)} %copy.55), channel_id=1, source_target_pairs={{0,4},{4,8},{8,12},{1,5},{5,9},{9,13},{2,6},{6,10},{10,14},{3,7},{... | collective-permute-start | bytes 27656 | tf_op jit(solution)/shard_map/ppermute | solution.py:14
  24.5 74.5 %collective-permute-start = (bf16[1,12,12,128]{3,0,2,1:T(2,128)(2,1)S(1)}, bf16[1,12,12,128]{3,0,2,1:T(2,128)(2,1)S(1)}, u32[]{:S(2)}, u32[]{:S(2)}) collective-permute-start(bf16[1,12,12,128]{3,0,2,1:T(2,128)(2,1)S(1)} %get-tuple-element.17), channel_id=1, source_target_pairs={{16,0},{0,16},{17,1},{1,17},{18,2},{2,18},{19,3},{3,19},{20,4},{4,... | collective-permute-start | bytes 110600 | tf_op jit(solution)/shard_map/ppermute | solution.py:15
  24.6 74.4 %collective-permute-start.1 = (bf16[1,12,12,128]{3,0,2,1:T(2,128)(2,1)S(1)}, bf16[1,12,12,128]{3,0,2,1:T(2,128)(2,1)S(1)}, u32[]{:S(2)}, u32[]{:S(2)}) collective-permute-start(bf16[1,12,12,128]{3,0,2,1:T(2,128)(2,1)S(1)} %get-tuple-element.18), channel_id=1, source_target_pairs={{0,16},{16,0},{1,17},{17,1},{2,18},{18,2},{3,19},{19,3},{4,20},{20... | collective-permute-start | bytes 110600 | tf_op jit(solution)/shard_map/ppermute | solution.py:14
  25.1 10.2 %copy-start.6 = (bf16[32,36,128]{2,0,1:T(8,128)(2,1)S(1)}, bf16[32,36,128]{2,0,1:T(8,128)(2,1)}, u32[]{:S(2)}) copy-start(bf16[32,36,128]{2,0,1:T(8,128)(2,1)} %param.15) | copy-start | bytes 884740
  35.3 5.5 %copy-start.3 = (bf16[32,6,12,128]{3,0,2,1:T(8,128)(2,1)S(1)}, bf16[32,6,12,128]{3,0,2,1:T(8,128)(2,1)}, u32[]{:S(2)}) copy-start(bf16[32,6,12,128]{3,0,2,1:T(8,128)(2,1)} %param.9) | copy-start | bytes 1769476
  35.3 5.5 %copy-start.4 = (bf16[32,6,12,128]{3,0,2,1:T(8,128)(2,1)S(1)}, bf16[32,6,12,128]{3,0,2,1:T(8,128)(2,1)}, u32[]{:S(2)}) copy-start(bf16[32,6,12,128]{3,0,2,1:T(8,128)(2,1)} %param.12) | copy-start | bytes 1769476
  54.2 43.1 %all-to-all-start.1 = ((bf16[8,12,48,128]{3,0,1,2:T(8,128)(2,1)}), bf16[8,12,48,128]{3,0,1,2:T(8,128)(2,1)}, u32[]{:S(2)}, u32[]{:S(2)}) async-start(bf16[8,12,48,128]{3,0,1,2:T(8,128)(2,1)} %copy.47), calls=%async_computation.1 | async-start | bytes 2359296 | tf_op jit(solution)/shard_map/all_to_all | solution.py:47
  58.7 20.0 %copy-start.7 = (f32[6]{0:T(128)S(1)}, f32[6]{0:T(128)}, u32[]{:S(2)}) copy-start(f32[6]{0:T(128)} %param.17) | copy-start | bytes 76
  97.3 1.7 %copy-start.2 = (bf16[32,12,12,1]{3,0,2,1:T(8,128)(2,1)S(1)}, bf16[32,12,12,1]{3,0,2,1:T(8,128)(2,1)}, u32[]{:S(2)}) copy-start(bf16[32,12,12,1]{3,0,2,1:T(8,128)(2,1)} %copy.56) | copy-start | bytes 27652
  103.8 1.3 copy-start.5
  103.8 47.1 %copy-start.1 = (bf16[288,288]{1,0:T(8,128)(2,1)S(1)}, bf16[288,288]{1,0:T(8,128)(2,1)}, u32[]{:S(2)}) copy-start(bf16[288,288]{1,0:T(8,128)(2,1)} %param.16) | copy-start | bytes 497668
where the time goes:
time: 152 us; the launch traced here: 151 us
  local copies, waits for them, and re-layouts  48.4 us (32%)
  blocking collectives  40.9 us (27%)
  matrix products  20.8 us (14%)
  starting transfers between devices  17.2 us (11%)
  other arithmetic  12.6 us (8%)
  waiting for transfers between devices  7.02 us (5%)
  between operations  3.94 us (3%)
    psum x1, blocking collectives, body(): lax.psum((norm_b, norm_c, value_c, value_a, value_e), ('tx', 'ty', 'lz'))  40.9 us
    dot_general x1, matrix products, body(): jnp.einsum('xuwy,xfwzy->xfuzy', blocks, stacked.reshape(rows_here, 2, uni...  20 us
    transpose x1, local copies, waits for them, and re-layouts, body(): jnp.einsum('xuwy,xfwzy->xfuzy', blocks, stacked.reshape(rows_here, 2, uni...  15.6 us
    reshape x1, local copies, waits for them, and re-layouts, body(): stacked.reshape(rows_here, 2, units, layers, cells)  10.2 us
    all_to_all x1, waiting for transfers between devices, body(): lax.all_to_all(stacked, 'lz', split_axis=0, concat_axis=2, tiled=True)  7.01 us
    all_to_all x1, starting transfers between devices, body(): lax.all_to_all(stacked, 'lz', split_axis=0, concat_axis=2, tiled=True)  6.35 us
    reshape x1, local copies, waits for them, and re-layouts, body(): blocks = cell_blocks.reshape(rows_here, units, units, cells)  5.47 us
    ppermute x2, starting transfers between devices, extended(): before = lax.ppermute(last, axis, up)  5.05 us
  transfers between devices with their start and end apart: 6, of which 1 were waited for; matrix products, arithmetic and copies ran while one was open for 46% of the time, Pallas kernels for 0%

commit v1 on v0

--- a/solution.py
+++ b/solution.py
@@ -71,7 +71,7 @@
     value_a = jnp.sum(column_b * test_full)
     value_e = jnp.sum(column_b * dir_full)
     norm_b, norm_c, value_c, value_a, value_e = lax.psum(
-        (norm_b, norm_c, value_c, value_a, value_e), ("tx", "ty", "lz")
+        lax.psum((norm_b, norm_c, value_c, value_a, value_e), ("ty", "lz")), "tx"
     )
     border = jnp.stack(
         [value_a / jnp.sqrt(norm_b), value_e / jnp.sqrt(norm_b), value_c / jnp.sqrt(norm_c)]

time: 152 us -> 157 us (1.033)
  blocking collectives: 40.9 us -> 46 us
    psum x1 -> x2, blocking collectives: 40.9 us -> 46 us  [the longest x1 42.9 us: body(): lax.psum((norm_b, norm_c, value_c, value_a, value_e), ('ty', 'lz'))]
  transfers between devices with their start and end apart: 6 -> 6, of which waited for: 1 -> 1; matrix products, arithmetic and copies ran while one was open for 46% -> 44% of each run, Pallas kernels for 0% -> 0%
where the time goes in v1:
time: 157 us; the launch traced here: 156 us
  local copies, waits for them, and re-layouts  48.3 us (31%)
  blocking collectives  46 us (29%)
  matrix products  20.8 us (13%)
  starting transfers between devices  17.2 us (11%)
  other arithmetic  12.6 us (8%)
  waiting for transfers between devices  7.02 us (4%)
  between operations  4.02 us (3%)
    psum x1, blocking collectives, body(): lax.psum((norm_b, norm_c, value_c, value_a, value_e), ('ty', 'lz'))  42.9 us
    dot_general x1, matrix products, body(): jnp.einsum('xuwy,xfwzy->xfuzy', blocks, stacked.reshape(rows_here, 2, uni...  20 us
    transpose x1, local copies, waits for them, and re-layouts, body(): jnp.einsum('xuwy,xfwzy->xfuzy', blocks, stacked.reshape(rows_here, 2, uni...  15.6 us
    reshape x1, local copies, waits for them, and re-layouts, body(): stacked.reshape(rows_here, 2, units, layers, cells)  10.2 us
    all_to_all x1, waiting for transfers between devices, body(): lax.all_to_all(stacked, 'lz', split_axis=0, concat_axis=2, tiled=True)  7.01 us
    all_to_all x1, starting transfers between devices, body(): lax.all_to_all(stacked, 'lz', split_axis=0, concat_axis=2, tiled=True)  6.35 us
    reshape x1, local copies, waits for them, and re-layouts, body(): blocks = cell_blocks.reshape(rows_here, units, units, cells)  5.45 us
    ppermute x2, starting transfers between devices, extended(): before = lax.ppermute(last, axis, up)  5.05 us
  transfers between devices with their start and end apart: 6, of which 1 were waited for; matrix products, arithmetic and copies ran while one was open for 44% of the time, Pallas kernels for 0%

profile of v1, /device:TPU:0, one launch (start us, length us, event | category | flops | bytes accessed | tf_op | source)
XLA Modules:
  0.0 156.0 jit_solution(4730552528013998270)
XLA Ops:
  2.3 1.3 broadcast_multiply_fusion.1
  3.7 1.7 %copy.43 = bf16[32,12,12,128]{3,2,1,0:T(8,128)(2,1)} copy(bf16[32,12,12,128]{3,0,2,1:T(8,128)(2,1)S(1)} %pad_maximum_fusion) | data formatting | bytes 2359296 | tf_op jit(solution)/shard_map/concatenate | solution.py:29
  5.4 6.3 %all-to-all-start = ((bf16[32,12,12,128]{3,2,1,0:T(8,128)(2,1)}), bf16[32,12,12,128]{3,2,1,0:T(8,128)(2,1)}, u32[]{:S(2)}, u32[]{:S(2)}) async-start(bf16[32,12,12,128]{3,2,1,0:T(8,128)(2,1)} %copy.43), calls=%async_computation | async-start | bytes 3145728 | tf_op jit(solution)/shard_map/all_to_all | solution.py:41
  11.7 1.9 %fusion.7 = (bf16[32,12,12,1]{3,0,2,1:T(8,128)(2,1)}, bf16[32,12,12,1]{3,0,2,1:T(8,128)(2,1)}) fusion(bf16[32,6,12,128]{3,0,2,1:T(8,128)(2,1)S(1)} %get-tuple-element.26, bf16[32,6,12,128]{3,0,2,1:T(8,128)(2,1)S(1)} %get-tuple-element.27), kind=kLoop, calls=%fused_computation.25 | loop fusion | flops 9216 | bytes 1198080 | tf_op jit(solution)/shard_map/concatenate | solution.py:29
  13.6 2.4 %copy.53 = bf16[32,12,12,1]{0,2,3,1:T(8,128)(2,1)S(1)} copy(bf16[32,12,12,1]{3,0,2,1:T(8,128)(2,1)} %get-tuple-element.24) | data formatting | bytes 18432 | tf_op jit(solution)/shard_map/slice | solution.py:13
  16.0 1.3 collective-permute-start.2
  17.3 2.5 %copy.55 = bf16[32,12,12,1]{0,2,3,1:T(8,128)(2,1)S(1)} copy(bf16[32,12,12,1]{3,0,2,1:T(8,128)(2,1)} %get-tuple-element.25) | data formatting | bytes 18432 | tf_op jit(solution)/shard_map/slice | solution.py:12
  19.8 4.6 %collective-permute-start.3 = (bf16[32,12,12,1]{0,2,3,1:T(8,128)(2,1)S(1)}, bf16[32,12,12,1]{0,2,3,1:T(8,128)(2,1)S(1)}, u32[]{:S(2)}, u32[]{:S(2)}) collective-permute-start(bf16[32,12,12,1]{0,2,3,1:T(8,128)(2,1)S(1)} %copy.55), channel_id=1, source_target_pairs={{0,4},{4,8},{8,12},{1,5},{5,9},{9,13},{2,6},{6,10},{10,14},{3,7},{... | collective-permute-start | bytes 27656 | tf_op jit(solution)/shard_map/ppermute | solution.py:14
  25.1 10.2 %copy.50 = bf16[32,2,6,12,128]{3,2,1,4,0:T(8,128)(2,1)} copy(bf16[32,2,6,12,128]{4,0,3,2,1:T(8,128)(2,1)S(1)} %bitcast.37) | data formatting | bytes 2359296 | tf_op jit(solution)/shard_map/reshape | solution.py:65
  35.3 5.5 %copy.58 = bf16[32,6,6,128,1]{2,1,4,3,0:T(8,128)(2,1)} copy(bf16[32,6,6,128,1]{3,0,2,1,4:T(8,128)(2,1)S(1)} %bitcast.41) | data formatting | bytes 589824 | tf_op jit(solution)/shard_map/reshape | solution.py:61
  40.7 1.0 fusion.3
  41.8 7.0 %all-to-all-done = bf16[32,12,12,128]{3,2,1,0:T(8,128)(2,1)} async-done(((bf16[32,12,12,128]{3,2,1,0:T(8,128)(2,1)}), bf16[32,12,12,128]{3,2,1,0:T(8,128)(2,1)}, u32[]{:S(2)}, u32[]{:S(2)}) %all-to-all-start) | async-done | bytes 1179680 | tf_op jit(solution)/shard_map/all_to_all | solution.py:41
  48.8 2.8 %copy.45 = bf16[8,12,4,12,128]{4,0,3,2,1:T(8,128)(2,1)S(1)} copy(bf16[8,12,4,12,128]{4,3,1,0,2:T(8,128)(2,1)} %bitcast.3) | data formatting | bytes 2359296 | tf_op jit(solution)/shard_map/all_to_all | solution.py:41
  52.3 1.9 %copy.47 = bf16[8,12,48,128]{3,0,1,2:T(8,128)(2,1)} copy(bf16[8,12,48,128]{3,2,1,0:T(8,128)(2,1)S(1)} %bitcast.39) | data formatting | bytes 2359296 | tf_op jit(solution)/shard_map/reshape | solution.py:46
  54.2 4.5 %all-to-all-start.1 = ((bf16[8,12,48,128]{3,0,1,2:T(8,128)(2,1)}), bf16[8,12,48,128]{3,0,1,2:T(8,128)(2,1)}, u32[]{:S(2)}, u32[]{:S(2)}) async-start(bf16[8,12,48,128]{3,0,1,2:T(8,128)(2,1)} %copy.47), calls=%async_computation.1 | async-start | bytes 2359296 | tf_op jit(solution)/shard_map/all_to_all | solution.py:47
  58.7 20.0 %convolution_bitcast_fusion = f32[32,2,6,12,128]{3,2,1,4,0:T(8,128)} fusion(bf16[32,2,6,12,128]{3,2,1,4,0:T(8,128)(2,1)} %copy.50, bf16[32,6,6,128,1]{2,1,4,3,0:T(8,128)(2,1)} %copy.58), kind=kOutput, calls=%fused_computation | convolution fusion | flops 7077888 | bytes 3833856 | tf_op jit(solution)/shard_map/xuwy,xfwzy->xfuzy/dot_general | solution.py:62
  78.8 15.6 %copy.52 = f32[32,2,6,12,128]{4,0,3,2,1:T(8,128)} copy(f32[32,2,6,12,128]{3,2,1,4,0:T(8,128)} %convolution_bitcast_fusion) | data formatting | bytes 4718592 | tf_op jit(solution)/shard_map/xuwy,xfwzy->xfuzy/transpose | solution.py:62
  95.4 1.9 %copy.56 = bf16[32,12,12,1]{3,0,2,1:T(8,128)(2,1)} copy(bf16[32,12,12,1]{0,2,3,1:T(8,128)(2,1)S(1)} %collective-permute-done.3) | data formatting | bytes 18432 | tf_op jit(solution)/shard_map/ppermute | solution.py:14
  97.3 1.6 %copy.48 = bf16[8,12,48,128]{3,0,2,1:T(8,128)(2,1)S(1)} copy(bf16[8,12,48,128]{3,0,1,2:T(8,128)(2,1)} %all-to-all-done.1) | data formatting | bytes 2359296 | tf_op jit(solution)/shard_map/all_to_all | solution.py:47
  99.0 4.8 %fusion.1 = f32[32,12,12,128]{3,0,2,1:T(8,128)S(1)} fusion(f32[32,2,6,12,128]{4,0,3,2,1:T(8,128)} %copy.52, bf16[32,12,12,1]{3,0,2,1:T(8,128)(2,1)S(1)} %copy-done.2, bf16[32,6,12,128]{3,0,2,1:T(8,128)(2,1)S(1)} %get-tuple-element.27, bf16[32,6,12,128]{3,0,2,1:T(8,128)(2,1)S(1)} %get-tuple-element.26, bf16[32,12,12,1]{3,0,2,1:T(8,128)(2,1)S(1)} %copy.54, ...), kind=kLoop, calls=%fused_computation.4 | loop fusion | flops 22413312 | bytes 7186480 | tf_op jit(solution)/shard_map/mul | solution.py:68
  103.8 1.3 fusion.15
  105.1 1.0 fusion.4
  106.1 42.9 %all-reduce = (f32[]{:T(128)}, f32[]{:T(128)}, f32[]{:T(128)}, f32[]{:T(128)}, f32[]{:T(128)}) all-reduce(f32[]{:T(128)} %get-tuple-element.7, f32[]{:T(128)} %get-tuple-element.6, f32[]{:T(128)} %get-tuple-element.4, f32[]{:T(128)} %get-tuple-element.5, f32[]{:T(128)} %get-tuple-element.3), channel_id=1, replica_groups=mesh['tx'=2,'ty'=4,'lz'=4] {'ty','lz'}, use_global_device_ids=true, to_apply=%region_11.0 | all-reduce | flops 5 | bytes 40 | tf_op jit(solution)/shard_map/psum | solution.py:74
  149.0 3.2 %all-reduce.1 = (f32[]{:T(128)}, f32[]{:T(128)}, f32[]{:T(128)}, f32[]{:T(128)}, f32[]{:T(128)}) all-reduce(f32[]{:T(128)} %get-tuple-element.8, f32[]{:T(128)} %get-tuple-element.9, f32[]{:T(128)} %get-tuple-element.10, f32[]{:T(128)} %get-tuple-element.11, f32[]{:T(128)} %get-tuple-element.12), channel_id=1, replica_groups=mesh['tx'=2,'ty'=4,'lz'=4] {'tx'}, use_global_device_ids=true, to_apply=%region_12.0 | all-reduce | flops 5 | bytes 40 | tf_op jit(solution)/shard_map/psum | solution.py:73
  (32 shorter events, 4.9 us)
Async XLA Ops:
  0.6 50.9 %copy-start = (bf16[288,288]{1,0:T(8,128)(2,1)S(1)}, bf16[288,288]{1,0:T(8,128)(2,1)}, u32[]{:S(2)}) copy-start(bf16[288,288]{1,0:T(8,128)(2,1)} %param.16) | copy-start | bytes 497668
  5.4 43.4 %all-to-all-start = ((bf16[32,12,12,128]{3,2,1,0:T(8,128)(2,1)}), bf16[32,12,12,128]{3,2,1,0:T(8,128)(2,1)}, u32[]{:S(2)}, u32[]{:S(2)}) async-start(bf16[32,12,12,128]{3,2,1,0:T(8,128)(2,1)} %copy.43), calls=%async_computation | async-start | bytes 3145728 | tf_op jit(solution)/shard_map/all_to_all | solution.py:41
  16.0 78.4 %collective-permute-start.2 = (bf16[32,12,12,1]{0,2,3,1:T(8,128)(2,1)S(1)}, bf16[32,12,12,1]{0,2,3,1:T(8,128)(2,1)S(1)}, u32[]{:S(2)}, u32[]{:S(2)}) collective-permute-start(bf16[32,12,12,1]{0,2,3,1:T(8,128)(2,1)S(1)} %copy.53), channel_id=1, source_target_pairs={{4,0},{8,4},{12,8},{5,1},{9,5},{13,9},{6,2},{10,6},{14,10},{7,3},{... | collective-permute-start | bytes 27656 | tf_op jit(solution)/shard_map/ppermute | solution.py:15
  19.8 75.6 %collective-permute-start.3 = (bf16[32,12,12,1]{0,2,3,1:T(8,128)(2,1)S(1)}, bf16[32,12,12,1]{0,2,3,1:T(8,128)(2,1)S(1)}, u32[]{:S(2)}, u32[]{:S(2)}) collective-permute-start(bf16[32,12,12,1]{0,2,3,1:T(8,128)(2,1)S(1)} %copy.55), channel_id=1, source_target_pairs={{0,4},{4,8},{8,12},{1,5},{5,9},{9,13},{2,6},{6,10},{10,14},{3,7},{... | collective-permute-start | bytes 27656 | tf_op jit(solution)/shard_map/ppermute | solution.py:14
  24.5 74.4 %collective-permute-start = (bf16[1,12,12,128]{3,0,2,1:T(2,128)(2,1)S(1)}, bf16[1,12,12,128]{3,0,2,1:T(2,128)(2,1)S(1)}, u32[]{:S(2)}, u32[]{:S(2)}) collective-permute-start(bf16[1,12,12,128]{3,0,2,1:T(2,128)(2,1)S(1)} %get-tuple-element.22), channel_id=1, source_target_pairs={{16,0},{0,16},{17,1},{1,17},{18,2},{2,18},{19,3},{3,19},{20,4},{4,... | collective-permute-start | bytes 110600 | tf_op jit(solution)/shard_map/ppermute | solution.py:15
  24.6 74.4 %collective-permute-start.1 = (bf16[1,12,12,128]{3,0,2,1:T(2,128)(2,1)S(1)}, bf16[1,12,12,128]{3,0,2,1:T(2,128)(2,1)S(1)}, u32[]{:S(2)}, u32[]{:S(2)}) collective-permute-start(bf16[1,12,12,128]{3,0,2,1:T(2,128)(2,1)S(1)} %get-tuple-element.23), channel_id=1, source_target_pairs={{0,16},{16,0},{1,17},{17,1},{2,18},{18,2},{3,19},{19,3},{4,20},{20... | collective-permute-start | bytes 110600 | tf_op jit(solution)/shard_map/ppermute | solution.py:14
  25.1 10.2 %copy-start.6 = (bf16[32,36,128]{2,0,1:T(8,128)(2,1)S(1)}, bf16[32,36,128]{2,0,1:T(8,128)(2,1)}, u32[]{:S(2)}) copy-start(bf16[32,36,128]{2,0,1:T(8,128)(2,1)} %param.15) | copy-start | bytes 884740
  35.3 5.5 %copy-start.3 = (bf16[32,6,12,128]{3,0,2,1:T(8,128)(2,1)S(1)}, bf16[32,6,12,128]{3,0,2,1:T(8,128)(2,1)}, u32[]{:S(2)}) copy-start(bf16[32,6,12,128]{3,0,2,1:T(8,128)(2,1)} %param.9) | copy-start | bytes 1769476
  35.3 5.5 %copy-start.4 = (bf16[32,6,12,128]{3,0,2,1:T(8,128)(2,1)S(1)}, bf16[32,6,12,128]{3,0,2,1:T(8,128)(2,1)}, u32[]{:S(2)}) copy-start(bf16[32,6,12,128]{3,0,2,1:T(8,128)(2,1)} %param.12) | copy-start | bytes 1769476
  54.2 43.1 %all-to-all-start.1 = ((bf16[8,12,48,128]{3,0,1,2:T(8,128)(2,1)}), bf16[8,12,48,128]{3,0,1,2:T(8,128)(2,1)}, u32[]{:S(2)}, u32[]{:S(2)}) async-start(bf16[8,12,48,128]{3,0,1,2:T(8,128)(2,1)} %copy.47), calls=%async_computation.1 | async-start | bytes 2359296 | tf_op jit(solution)/shard_map/all_to_all | solution.py:47
  58.7 20.0 %copy-start.7 = (f32[6]{0:T(128)S(1)}, f32[6]{0:T(128)}, u32[]{:S(2)}) copy-start(f32[6]{0:T(128)} %param.17) | copy-start | bytes 76
  97.3 1.7 %copy-start.2 = (bf16[32,12,12,1]{3,0,2,1:T(8,128)(2,1)S(1)}, bf16[32,12,12,1]{3,0,2,1:T(8,128)(2,1)}, u32[]{:S(2)}) copy-start(bf16[32,12,12,1]{3,0,2,1:T(8,128)(2,1)} %copy.56) | copy-start | bytes 27652
  103.8 1.3 copy-start.5
  103.8 52.2 %copy-start.1 = (bf16[288,288]{1,0:T(8,128)(2,1)S(1)}, bf16[288,288]{1,0:T(8,128)(2,1)}, u32[]{:S(2)}) copy-start(bf16[288,288]{1,0:T(8,128)(2,1)} %param.16) | copy-start | bytes 497668
